TPU v7x, 32 devices: a whole 2x2x4 slice. The times are simulated.
32 devices in a mesh: region: 4 (over z), seq: 8 (over y, x, core).
Axes of the slice: x: 2, y: 2, z: 4, core: 2. Of those that a mesh axis runs over, the one named last changes fastest.
Arguments:
- queries: bfloat16 [4096, 1024], P(('region', 'seq')), may hold values from -80 to 80
- keys: bfloat16 [4096, 1024], P(('region', 'seq')), may hold values from -8 to 8
- values: bfloat16 [4096, 1024], P(('region', 'seq')), may hold values from -6 to 6
- out_grad: bfloat16 [4096, 1024], P(('region', 'seq')), may hold values from -6 to 6
- table: int32 [4, 8, 8], P('region'), may hold values from -1 to 23, as said below
- counts: int32 [4, 8], replicated, may hold values from 2 to 128
- sendlist: int32 [4, 2, 8], replicated, may hold values from 0 to 7, as said below
Outputs:
- attended: bfloat16 [4096, 1024], P(('region', 'seq'))
- query_grad: bfloat16 [4096, 1024], P(('region', 'seq'))
- key_grad: bfloat16 [4096, 1024], P(('region', 'seq'))
- value_grad: bfloat16 [4096, 1024], P(('region', 'seq'))
Inputs may be any that keep to these rules, and one draw needn't show every extreme that they name: `table`: entry 0 of a block is the block itself; entries of one block differ; -1 marks padding and only follows live entries; an entry of 8 or more names boundary slot entry - 8 of key_ext. `sendlist`: the 8 blocks of one list differ.
All inputs are finite; a program needn't handle non-finite values.
Results may differ from a plain program's by a relative error of at most 0.035.
Values may be sent and summed in bfloat16 or wider, within the bound.
A program may use at most 128 MiB of HBM per device.

v0:
```python
from functools import partial
import math

import jax
import jax.numpy as jnp
from jax import lax
from jax.sharding import PartitionSpec as P

H = 16
HD = 64
BLK = 128
NBR = 8
BND = 8


def with_halo(cells, sides, width):
    for axis, dim in sides:
        count = lax.axis_size(axis)
        head = lax.slice_in_dim(cells, 0, width, axis=dim)
        tail = lax.slice_in_dim(cells, cells.shape[dim] - width, cells.shape[dim], axis=dim)
        cells = jnp.concatenate(
            [
                lax.ppermute(tail, axis, [(i, (i + 1) % count) for i in range(count)]),
                cells,
                lax.ppermute(head, axis, [((i + 1) % count, i) for i in range(count)]),
            ],
            axis=dim,
        )
    return cells


def attend_group(carry, inputs, key_ext, value_ext, count_ext, scale):
    key_acc, value_acc = carry
    query_grp, grad_grp, table_grp, count_grp, offset_grp = inputs
    group_size, neighbours = table_grp.shape
    heads = query_grp.shape[1]
    piece_len = query_grp.shape[2]
    depth = query_grp.shape[3]
    block_len = key_ext.shape[2]
    safe_ids = jnp.maximum(table_grp, 0)
    key_rows = key_ext[:, safe_ids].reshape(heads, group_size, neighbours * block_len, depth)
    value_rows = value_ext[:, safe_ids].reshape(heads, group_size, neighbours * block_len, depth)
    positions = jnp.arange(block_len, dtype=jnp.int32)
    key_valid = (table_grp >= 0)[:, :, None] & (
        positions[None, None, :] < count_ext[safe_ids][:, :, None]
    )
    key_valid = key_valid.reshape(group_size, neighbours * block_len)
    query_pos = jnp.arange(piece_len, dtype=jnp.int32)
    query_valid = offset_grp[:, None] + query_pos[None, :] < count_grp[:, None]
    scores = (
        jnp.einsum("bhqe,hbke->bhqk", query_grp, key_rows, preferred_element_type=jnp.float32)
        * scale
    )
    scores = jnp.where(key_valid[:, None, None, :], scores, jnp.float32(-1e30))
    peak = jnp.max(scores, axis=-1, keepdims=True)
    expo = jnp.exp(scores - peak)
    prob = (expo / jnp.sum(expo, axis=-1, keepdims=True)).astype(jnp.bfloat16)
    attended = jnp.einsum("bhqk,hbke->bhqe", prob, value_rows, preferred_element_type=jnp.float32)
    attended = jnp.where(query_valid[:, None, :, None], attended, jnp.float32(0.0)).astype(
        jnp.bfloat16
    )
    grad_masked = jnp.where(query_valid[:, None, :, None], grad_grp, jnp.zeros_like(grad_grp))
    dprob = jnp.einsum(
        "bhqe,hbke->bhqk", grad_masked, value_rows, preferred_element_type=jnp.float32
    )
    delta = jnp.sum(grad_masked.astype(jnp.float32) * attended.astype(jnp.float32), axis=-1)[
        ..., None
    ]
    dscore = (prob.astype(jnp.float32) * (dprob - delta)).astype(jnp.bfloat16)
    query_grad = (
        jnp.einsum("bhqk,hbke->bhqe", dscore, key_rows, preferred_element_type=jnp.float32) * scale
    )
    query_grad = query_grad.astype(jnp.bfloat16)
    key_part = (
        jnp.einsum("bhqk,bhqe->hbke", dscore, query_grp, preferred_element_type=jnp.float32) * scale
    )
    value_part = jnp.einsum(
        "bhqk,bhqe->hbke", prob, grad_masked, preferred_element_type=jnp.float32
    )
    flat_ids = safe_ids.reshape(-1)
    key_acc = key_acc.at[:, flat_ids].add(
        key_part.reshape(heads, group_size * neighbours, block_len, depth)
    )
    value_acc = value_acc.at[:, flat_ids].add(
        value_part.reshape(heads, group_size * neighbours, block_len, depth)
    )
    return ((key_acc, value_acc), (attended, query_grad))


def body(queries, keys, values, out_grad, table, counts, sendlist):
    seq_count = lax.axis_size("seq")
    region_count = lax.axis_size("region")
    galaxies, width = queries.shape
    pair_count = seq_count // 2
    pair_heads = 2 * H // seq_count
    pair_width = pair_heads * HD
    half_rows = galaxies // 2
    region_rows = seq_count * galaxies
    block_total = region_rows // BLK
    parity = lax.axis_index("seq") % 2
    region_now = lax.axis_index("region")

    def half_slots(matrix):
        return (
            matrix.reshape(2, half_rows, pair_count, pair_width)
            .transpose(2, 0, 1, 3)
            .reshape(seq_count, half_rows, pair_width)
        )

    query_heads, grad_heads = (
        lax.all_to_all(half_slots(queries), "seq", split_axis=0, concat_axis=1, tiled=True),
        lax.all_to_all(half_slots(out_grad), "seq", split_axis=0, concat_axis=1, tiled=True),
    )

    def all_slots(matrix):
        grouped = matrix.reshape(galaxies, pair_count, pair_width).transpose(1, 0, 2)
        return jnp.repeat(grouped, 2, axis=0)

    key_heads, value_heads = (
        lax.all_to_all(all_slots(keys), "seq", split_axis=0, concat_axis=1, tiled=True),
        lax.all_to_all(all_slots(values), "seq", split_axis=0, concat_axis=1, tiled=True),
    )
    paired = jnp.stack([key_heads[0], value_heads[0]])
    head_first = paired.reshape(2, region_rows, pair_heads, HD).transpose(0, 2, 1, 3)
    head_blocks = head_first.reshape(2, pair_heads, block_total, BLK, HD)
    my_lists = sendlist[region_now]
    prev_ids = my_lists[0]
    next_ids = my_lists[1]
    rim_rows = BND * BLK
    packed_rim = rim_rows // 2
    outgoing = jnp.concatenate(
        [head_blocks[:, :, prev_ids], head_blocks[:, :, next_ids]], axis=2
    ).reshape(2, pair_heads, rim_rows, 2 * HD)
    widened = with_halo(outgoing, (("region", 2),), packed_rim)
    from_left = widened[:, :, :packed_rim].reshape(2, pair_heads, rim_rows, HD)
    from_right = widened[:, :, -packed_rim:].reshape(2, pair_heads, rim_rows, HD)
    slots = block_total + 2 * BND
    extended = jnp.concatenate([head_first, from_left, from_right], axis=2).reshape(
        2, pair_heads, slots, BLK, HD
    )
    left_region = (region_now + region_count - 1) % region_count
    right_region = (region_now + 1) % region_count
    count_ext = jnp.concatenate(
        [
            counts[region_now],
            counts[left_region][sendlist[left_region, 1]],
            counts[right_region][sendlist[right_region, 0]],
        ]
    )
    piece_rows = min(BLK, half_rows)
    per_source = half_rows // piece_rows
    piece_starts = (
        jnp.arange(seq_count, dtype=jnp.int32)[:, None] * galaxies
        + parity * half_rows
        + jnp.arange(per_source, dtype=jnp.int32)[None, :] * piece_rows
    ).reshape(-1)
    piece_blocks = piece_starts // BLK
    piece_offsets = piece_starts % BLK
    my_table = table[0][piece_blocks]
    my_counts = counts[region_now][piece_blocks]
    piece_total = seq_count * per_source
    group_width = 8
    groups = piece_total // group_width

    def scan_layout(matrix):
        return matrix.reshape(groups, group_width, piece_rows, pair_heads, HD).transpose(
            0, 1, 3, 2, 4
        )

    stepper = partial(
        attend_group,
        key_ext=extended[0],
        value_ext=extended[1],
        count_ext=count_ext,
        scale=1.0 / math.sqrt(HD),
    )
    start = (
        jnp.zeros((pair_heads, slots, BLK, HD), jnp.float32),
        jnp.zeros((pair_heads, slots, BLK, HD), jnp.float32),
    )
    carried, outputs = lax.scan(
        stepper,
        start,
        (
            scan_layout(query_heads),
            scan_layout(grad_heads),
            my_table.reshape(groups, group_width, NBR),
            my_counts.reshape(groups, group_width),
            piece_offsets.reshape(groups, group_width),
        ),
    )
    accum = jnp.stack([carried[0], carried[1]]).reshape(2, pair_heads, slots * BLK, HD)
    inner = accum[:, :, :region_rows].reshape(2, pair_heads, block_total, BLK, HD)
    rim_out = accum[:, :, region_rows:].reshape(2, pair_heads, rim_rows, 2 * HD)
    returned = with_halo(rim_out, (("region", 2),), packed_rim)
    back_left = returned[:, :, :packed_rim].reshape(2, pair_heads, BND, BLK, HD)
    back_right = returned[:, :, -packed_rim:].reshape(2, pair_heads, BND, BLK, HD)
    inner = inner.at[:, :, prev_ids].add(back_left)
    inner = inner.at[:, :, next_ids].add(back_right)
    inner = (
        inner.reshape(2, pair_heads, region_rows, HD)
        .transpose(0, 2, 1, 3)
        .reshape(2, region_rows, pair_width)
    )
    spread = lax.all_to_all(
        inner.reshape(2, seq_count, galaxies, pair_width),
        "seq",
        split_axis=1,
        concat_axis=1,
        tiled=True,
    )
    summed = spread.reshape(2, pair_count, 2, galaxies, pair_width).sum(axis=2)
    grads = summed.transpose(0, 2, 1, 3).reshape(2, galaxies, width)
    attended_heads = outputs[0].transpose(0, 1, 3, 2, 4).reshape(seq_count, half_rows, pair_width)
    qgrad_heads = outputs[1].transpose(0, 1, 3, 2, 4).reshape(seq_count, half_rows, pair_width)
    attended_back, qgrad_back = (
        lax.all_to_all(attended_heads, "seq", split_axis=0, concat_axis=0, tiled=True),
        lax.all_to_all(qgrad_heads, "seq", split_axis=0, concat_axis=0, tiled=True),
    )

    def owner_rows(received):
        return (
            received.reshape(pair_count, 2, half_rows, pair_width)
            .transpose(1, 2, 0, 3)
            .reshape(galaxies, width)
        )

    grads = grads.astype(jnp.bfloat16)
    return (owner_rows(attended_back), owner_rows(qgrad_back), grads[0], grads[1])


def solution(mesh):
    return jax.shard_map(
        body,
        mesh=mesh,
        in_specs=(
            P(("region", "seq"), None),
            P(("region", "seq"), None),
            P(("region", "seq"), None),
            P(("region", "seq"), None),
            P("region", None, None),
            P(),
            P(),
        ),
        out_specs=(
            P(("region", "seq"), None),
            P(("region", "seq"), None),
            P(("region", "seq"), None),
            P(("region", "seq"), None),
        ),
        check_vma=False,
    )
```

profile of v0, /device:TPU:0, one launch (start us, length us, event | category | flops | bytes accessed | tf_op | source)
XLA Modules:
  0.0 426.3 jit_solution(13458127873232549518)
XLA Ops:
  0.7 1.2 reshape.423
  3.0 5.2 %all-to-all-start.1 = ((bf16[8,128,256]{1,2,0:T(8,128)(2,1)}), bf16[8,128,256]{1,2,0:T(8,128)(2,1)S(1)}, u32[]{:S(2)}, u32[]{:S(2)}) async-start(bf16[8,128,256]{1,2,0:T(8,128)(2,1)} %bitcast.15), calls=%async_computation.1 | async-start | bytes 1048576 | tf_op jit(solution)/shard_map/all_to_all | solution.py:121
  11.1 6.8 %all-to-all-done.1 = bf16[8,128,256]{1,2,0:T(8,128)(2,1)S(1)} async-done(((bf16[8,128,256]{1,2,0:T(8,128)(2,1)}), bf16[8,128,256]{1,2,0:T(8,128)(2,1)S(1)}, u32[]{:S(2)}, u32[]{:S(2)}) %all-to-all-start.1) | async-done | bytes 524320 | tf_op jit(solution)/shard_map/all_to_all | solution.py:121
  18.7 3.5 all-to-all-start
  25.1 6.8 %all-to-all-done = bf16[8,128,256]{1,2,0:T(8,128)(2,1)S(1)} async-done(((bf16[8,128,256]{1,2,0:T(8,128)(2,1)}), bf16[8,128,256]{1,2,0:T(8,128)(2,1)S(1)}, u32[]{:S(2)}, u32[]{:S(2)}) %all-to-all-start) | async-done | bytes 524320 | tf_op jit(solution)/shard_map/all_to_all | solution.py:120
  31.9 3.4 all-to-all-start.4
  38.8 1.5 pad_maximum_fusion.1
  40.4 4.8 %copy.175 = bf16[2,4,16,128,64]{4,3,2,1,0:T(8,128)(2,1)} copy(bf16[2,4,16,128,64]{3,4,1,0,2:T(8,128)(2,1)} %pad_maximum_fusion.1) | data formatting | bytes 4194304 | tf_op jit(solution)/shard_map/concatenate | solution.py:131
  45.2 5.0 %reshape.426 = bf16[2,4,1024,128]{3,2,1,0:T(8,128)(2,1)S(1)} reshape(bf16[2,4,16,128,64]{4,3,2,1,0:T(8,128)(2,1)} %copy.175) | data formatting | bytes 4194304 | tf_op jit(solution)/shard_map/reshape | solution.py:133
  50.2 1.5 fusion.66
  51.7 3.6 collective-permute-start.1
  59.3 4.3 %all-to-all-start.2 = ((bf16[8,64,256]{2,1,0:T(8,128)(2,1)}), bf16[8,64,256]{2,1,0:T(8,128)(2,1)S(1)}, u32[]{:S(2)}, u32[]{:S(2)}) async-start(bf16[8,64,256]{2,1,0:T(8,128)(2,1)} %bitcast.26), calls=%async_computation.2 | async-start | bytes 524288 | tf_op jit(solution)/shard_map/all_to_all | solution.py:111
  65.9 4.6 %all-to-all-done.2 = bf16[8,64,256]{2,1,0:T(8,128)(2,1)S(1)} async-done(((bf16[8,64,256]{2,1,0:T(8,128)(2,1)}), bf16[8,64,256]{2,1,0:T(8,128)(2,1)S(1)}, u32[]{:S(2)}, u32[]{:S(2)}) %all-to-all-start.2) | async-done | bytes 262176 | tf_op jit(solution)/shard_map/all_to_all | solution.py:111
  71.6 7.6 %collective-permute-done.1 = bf16[2,4,512,128]{3,2,1,0:T(8,128)(2,1)S(1)} collective-permute-done((bf16[2,4,512,128]{3,2,1,0:T(8,128)(2,1)}, bf16[2,4,512,128]{3,2,1,0:T(8,128)(2,1)S(1)}, u32[]{:S(2)}, u32[]{:S(2)}) %collective-permute-start.1) | collective-permute-done | bytes 1048608 | tf_op jit(solution)/shard_map/ppermute | solution.py:25
  80.1 1.6 copy.177
  81.7 20.3 %collective-permute-done = bf16[2,4,512,128]{3,2,1,0:T(8,128)(2,1)} collective-permute-done((bf16[2,4,512,128]{3,2,1,0:T(8,128)(2,1)}, bf16[2,4,512,128]{3,2,1,0:T(8,128)(2,1)}, u32[]{:S(2)}, u32[]{:S(2)}) %collective-permute-start) | collective-permute-done | bytes 1048608 | tf_op jit(solution)/shard_map/ppermute | solution.py:23
  102.0 2.7 reshape.427
  104.7 1.6 copy.176
  106.4 1.7 pad_maximum_fusion
  109.0 3.1 gather_fusion.7
  112.8 3.0 gather_fusion.8
  115.9 6.7 %fusion.11 = f32[8,4,1024,64]{2,3,1,0:T(8,128)} fusion(bf16[8,8,4,8,8,128]{5,4,3,2,1,0:T(8,128)(2,1)} %bitcast.216, bf16[1,8,64,4,64]{4,3,2,1,0:T(4,128)(2,1)S(1)} %copy-done.4), kind=kOutput, calls=%fused_computation.27 | convolution fusion | flops 268435456 | bytes 12845056 | tf_op jit(solution)/shard_map/while/body/eval_jaxpr/bhqe,hbke->bhqk/dot_general | solution.py:51
  122.5 8.4 %fusion.68 = (f32[8,4,64]{2,1,0:T(4,128)S(1)}, f32[8,4,64,1024]{3,2,1,0:T(8,128)S(1)}) fusion(f32[8,4,1024,64]{2,3,1,0:T(8,128)} %fusion.11, pred[8,1024]{1,0:T(8,128)(4,1)S(1)} %fusion.50), kind=kOutput, calls=%fused_computation.114 | output fusion | flops 12583935 | bytes 16793600 | tf_op jit(solution)/shard_map/while/body/eval_jaxpr/sub | solution.py:56
  133.3 2.0 multiply_reduce_fusion
  135.3 4.5 %fusion.13 = f32[4,8,1024,64]{2,3,1,0:T(8,128)} fusion(bf16[8,4,64,1024]{3,2,1,0:T(8,128)(2,1)S(1)} %divide_convert_fusion, bf16[8,4,64,64]{2,3,1,0:T(8,128)(2,1)S(1)} %get-tuple-element.35), kind=kOutput, calls=%fused_computation.29 | convolution fusion | flops 268435456 | bytes 12845056 | tf_op jit(solution)/shard_map/while/body/eval_jaxpr/bhqk,bhqe->hbke/dot_general | solution.py:77
  139.8 1.9 multiply_convert_fusion
  141.6 1.9 copy-done.3
  143.6 1.3 broadcast_multiply_fusion
  144.9 8.1 %copy.197 = f32[4,8,1024,64]{2,1,3,0:T(8,128)} copy(f32[4,8,1024,64]{2,3,1,0:T(8,128)S(1)} %broadcast_multiply_fusion) | data formatting | bytes 16777216 | tf_op jit(solution)/shard_map/while/body/eval_jaxpr/mul | solution.py:75
  153.0 9.6 %reshape.524 = f32[4,64,128,64]{2,1,3,0:T(8,128)} reshape(f32[4,8,1024,64]{2,1,3,0:T(8,128)} %copy.197) | data formatting | bytes 16777216 | tf_op jit(solution)/shard_map/while/body/eval_jaxpr/reshape | solution.py:82
  162.6 11.5 %copy.198 = f32[64,4,128,64]{2,3,1,0:T(8,128)} copy(f32[64,4,128,64]{2,0,3,1:T(8,128)} %bitcast.220) | data formatting | bytes 16777216 | tf_op jit(solution)/shard_map/while/body/eval_jaxpr/reshape | solution.py:82
  174.5 13.2 %scatter_fusion = f32[4,24,128,64]{2,3,1,0:T(8,128)S(1)} fusion(f32[4,24,128,64]{2,3,1,0:T(8,128)S(1)} %broadcast.273.clone, s32[64]{0:T(128)S(1)} %reshape.485, f32[64,4,128,64]{2,3,1,0:T(8,128)} %copy.198), kind=kCustom, calls=%fused_computation.9 | custom fusion | flops 2097152 | bytes 25166080 | tf_op jit(solution)/shard_map/while/body/eval_jaxpr/scatter-add | solution.py:81
  187.6 3.5 copy.199
  191.2 3.0 stack.19
  194.2 1.9 constant_dynamic-update-slice_fusion.1
  196.0 11.5 %copy.202 = f32[4,8,1024,64]{2,1,3,0:T(8,128)} copy(f32[4,8,1024,64]{2,3,1,0:T(8,128)} %fusion.13) | data formatting | bytes 16777216 | tf_op jit(solution)/shard_map/while/body/eval_jaxpr/bhqk,bhqe->hbke/dot_general | solution.py:77
  207.5 9.3 %reshape.532 = f32[4,64,128,64]{2,1,3,0:T(8,128)} reshape(f32[4,8,1024,64]{2,1,3,0:T(8,128)} %copy.202) | data formatting | bytes 16777216 | tf_op jit(solution)/shard_map/while/body/eval_jaxpr/reshape | solution.py:85
  216.8 11.5 %copy.203 = f32[64,4,128,64]{2,3,1,0:T(8,128)} copy(f32[64,4,128,64]{2,0,3,1:T(8,128)} %bitcast.221) | data formatting | bytes 16777216 | tf_op jit(solution)/shard_map/while/body/eval_jaxpr/reshape | solution.py:85
  228.7 13.4 %scatter_fusion.1 = f32[4,24,128,64]{2,3,1,0:T(8,128)S(1)} fusion(f32[4,24,128,64]{2,3,1,0:T(8,128)S(1)} %broadcast.273.clone.1, s32[64]{0:T(128)S(1)} %reshape.485, f32[64,4,128,64]{2,3,1,0:T(8,128)} %copy.203), kind=kCustom, calls=%fused_computation.10 | custom fusion | flops 2097152 | bytes 25166080 | tf_op jit(solution)/shard_map/while/body/eval_jaxpr/scatter-add | solution.py:84
  242.1 3.5 copy.204
  245.5 2.8 stack.20
  248.4 1.9 constant_dynamic-update-slice_fusion
  250.3 4.6 %slice.77 = f32[2,4,2048,64]{2,3,1,0:T(8,128)} slice(f32[2,4,3072,64]{2,3,1,0:T(8,128)} %constant_dynamic-update-slice_fusion), slice={[0:2], [0:4], [1024:3072], [0:64]} | slice | bytes 8388608 | tf_op jit(solution)/shard_map/slice | solution.py:194
  254.9 6.9 %copy.205 = f32[2,4,2048,64]{3,2,1,0:T(8,128)} copy(f32[2,4,2048,64]{2,3,1,0:T(8,128)} %slice.77) | data formatting | bytes 8388608 | tf_op jit(solution)/shard_map/slice | solution.py:194
  261.8 7.2 %reshape.446 = f32[2,4,1024,128]{3,2,1,0:T(8,128)} reshape(f32[2,4,2048,64]{3,2,1,0:T(8,128)} %copy.205) | data formatting | bytes 8388608 | tf_op jit(solution)/shard_map/reshape | solution.py:194
  269.1 4.8 %fusion.64 = (f32[2,4,512,128]{3,2,1,0:T(8,128)}, f32[2,4,512,128]{3,2,1,0:T(8,128)}) fusion(f32[2,4,1024,128]{3,2,1,0:T(8,128)} %reshape.446), kind=kLoop, calls=%fused_computation.110 | loop fusion | bytes 8388608 | tf_op jit(solution)/shard_map/slice | solution.py:19
  273.8 1.8 collective-permute-start.2
  275.6 2.0 collective-permute-start.3
  278.6 4.1 all-to-all-start.3
  282.7 4.7 %fusion.40 = bf16[1,8,64,4,64]{4,2,3,1,0:T(8,128)(2,1)S(1)} fusion(bf16[8,4,64,1024]{3,2,1,0:T(8,128)(2,1)} %copy-done.3, bf16[8,8,4,8,8,128]{5,4,3,2,1,0:T(8,128)(2,1)} %bitcast.217), kind=kOutput, calls=%fused_computation.51 | convolution fusion | flops 268697600 | bytes 8650752 | tf_op jit(solution)/shard_map/while/body/eval_jaxpr/bhqk,hbke->bhqe/dot_general | solution.py:71
  288.9 1.9 copy_bitcast_fusion.1
  290.8 33.7 %collective-permute-done.2 = f32[2,4,512,128]{3,2,1,0:T(8,128)} collective-permute-done((f32[2,4,512,128]{3,2,1,0:T(8,128)}, f32[2,4,512,128]{3,2,1,0:T(8,128)}, u32[]{:S(2)}, u32[]{:S(2)}) %collective-permute-start.2) | collective-permute-done | bytes 2097184 | tf_op jit(solution)/shard_map/ppermute | solution.py:23
  324.5 4.4 %reshape.540 = f32[2,4,8,128,64]{4,3,2,1,0:T(8,128)} reshape(f32[2,4,512,128]{3,2,1,0:T(8,128)} %collective-permute-done.2) | data formatting | bytes 4194304 | tf_op jit(solution)/shard_map/reshape | solution.py:196
  328.8 3.8 copy.207
  332.7 35.0 %collective-permute-done.3 = f32[2,4,512,128]{3,2,1,0:T(8,128)} collective-permute-done((f32[2,4,512,128]{3,2,1,0:T(8,128)}, f32[2,4,512,128]{3,2,1,0:T(8,128)}, u32[]{:S(2)}, u32[]{:S(2)}) %collective-permute-start.3) | collective-permute-done | bytes 2097184 | tf_op jit(solution)/shard_map/ppermute | solution.py:25
  367.7 4.4 %reshape.548 = f32[2,4,8,128,64]{4,3,2,1,0:T(8,128)} reshape(f32[2,4,512,128]{3,2,1,0:T(8,128)} %collective-permute-done.3) | data formatting | bytes 4194304 | tf_op jit(solution)/shard_map/reshape | solution.py:197
  372.0 3.8 copy.208
  375.9 3.5 scatter_fusion.2
  379.4 3.5 scatter_fusion.3
  382.9 3.6 all-to-all-start.5
  387.2 1.7 copy.210
  388.9 4.4 %all-to-all-done.5 = bf16[8,64,256]{2,1,0:T(8,128)(2,1)S(1)} async-done(((bf16[8,64,256]{2,1,0:T(8,128)(2,1)}), bf16[8,64,256]{2,1,0:T(8,128)(2,1)S(1)}, u32[]{:S(2)}, u32[]{:S(2)}) %all-to-all-start.5) | async-done | bytes 262176 | tf_op jit(solution)/shard_map/all_to_all | solution.py:218
  393.4 3.6 all-to-all-start.6
  398.9 24.6 %all-to-all-done.6 = f32[2,8,128,256]{2,3,0,1:T(8,128)S(1)} async-done(((f32[2,8,128,256]{2,3,0,1:T(8,128)}), f32[2,8,128,256]{2,3,0,1:T(8,128)S(1)}, u32[]{:S(2)}, u32[]{:S(2)}) %all-to-all-start.6) | async-done | bytes 2097184 | tf_op jit(solution)/shard_map/all_to_all | solution.py:205
  (97 shorter events, 31.5 us)
Async XLA Ops:
  0.6 23.2 %copy-start = (s32[1,8,8]{2,1,0:T(8,128)S(1)}, s32[1,8,8]{2,1,0:T(8,128)}, u32[]{:S(2)}) copy-start(s32[1,8,8]{2,1,0:T(8,128)} %param.11) | copy-start | bytes 772
  0.6 22.3 %copy-start.8 = (bf16[128,1024]{1,0:T(8,128)(2,1)S(1)}, bf16[128,1024]{1,0:T(8,128)(2,1)}, u32[]{:S(2)}) copy-start(bf16[128,1024]{1,0:T(8,128)(2,1)} %param.10) | copy-start | bytes 786436
  3.0 14.9 %all-to-all-start.1 = ((bf16[8,128,256]{1,2,0:T(8,128)(2,1)}), bf16[8,128,256]{1,2,0:T(8,128)(2,1)S(1)}, u32[]{:S(2)}, u32[]{:S(2)}) async-start(bf16[8,128,256]{1,2,0:T(8,128)(2,1)} %bitcast.15), calls=%async_computation.1 | async-start | bytes 1048576 | tf_op jit(solution)/shard_map/all_to_all | solution.py:121
  11.1 13.4 %copy-start.9 = (s32[8]{0:T(128)}, s32[8]{0:T(128)S(1)}, u32[]{:S(2)}) copy-start(s32[8]{0:T(128)S(1)} %get-tuple-element.65) | copy-start | bytes 100
  11.1 13.4 %copy-start.11 = (s32[8]{0:T(128)}, s32[8]{0:T(128)S(1)}, u32[]{:S(2)}) copy-start(s32[8]{0:T(128)S(1)} %get-tuple-element.64) | copy-start | bytes 100
  18.7 13.1 %all-to-all-start = ((bf16[8,128,256]{1,2,0:T(8,128)(2,1)}), bf16[8,128,256]{1,2,0:T(8,128)(2,1)S(1)}, u32[]{:S(2)}, u32[]{:S(2)}) async-start(bf16[8,128,256]{1,2,0:T(8,128)(2,1)} %bitcast.13), calls=%async_computation | async-start | bytes 1048576 | tf_op jit(solution)/shard_map/all_to_all | solution.py:120
  31.9 27.4 %all-to-all-start.4 = ((bf16[8,64,256]{2,1,0:T(8,128)(2,1)}), bf16[8,64,256]{2,1,0:T(8,128)(2,1)S(1)}, u32[]{:S(2)}, u32[]{:S(2)}) async-start(bf16[8,64,256]{2,1,0:T(8,128)(2,1)} %bitcast.38), calls=%async_computation.4 | async-start | bytes 524288 | tf_op jit(solution)/shard_map/all_to_all | solution.py:112
  51.7 27.5 %collective-permute-start.1 = (bf16[2,4,512,128]{3,2,1,0:T(8,128)(2,1)}, bf16[2,4,512,128]{3,2,1,0:T(8,128)(2,1)S(1)}, u32[]{:S(2)}, u32[]{:S(2)}) collective-permute-start(bf16[2,4,512,128]{3,2,1,0:T(8,128)(2,1)} %get-tuple-element.54), channel_id=1, source_target_pairs={{8,0},{16,8},{24,16},{0,24},{9,1},{17,9},{25,17},{1,25},{10,2},{18... | collective-permute-start | bytes 3145736 | tf_op jit(solution)/shard_map/ppermute | solution.py:25
  55.3 46.7 %collective-permute-start = (bf16[2,4,512,128]{3,2,1,0:T(8,128)(2,1)}, bf16[2,4,512,128]{3,2,1,0:T(8,128)(2,1)}, u32[]{:S(2)}, u32[]{:S(2)}) collective-permute-start(bf16[2,4,512,128]{3,2,1,0:T(8,128)(2,1)} %get-tuple-element.53), channel_id=1, source_target_pairs={{0,8},{8,16},{16,24},{24,0},{1,9},{9,17},{17,25},{25,1},{2,10},{10... | collective-permute-start | bytes 3145736 | tf_op jit(solution)/shard_map/ppermute | solution.py:23
  59.3 11.2 %all-to-all-start.2 = ((bf16[8,64,256]{2,1,0:T(8,128)(2,1)}), bf16[8,64,256]{2,1,0:T(8,128)(2,1)S(1)}, u32[]{:S(2)}, u32[]{:S(2)}) async-start(bf16[8,64,256]{2,1,0:T(8,128)(2,1)} %bitcast.26), calls=%async_computation.2 | async-start | bytes 524288 | tf_op jit(solution)/shard_map/all_to_all | solution.py:111
  80.1 26.3 %copy-start.5 = (bf16[2,4,1024,64]{2,3,1,0:T(8,128)(2,1)S(1)}, bf16[2,4,1024,64]{2,3,1,0:T(8,128)(2,1)}, u32[]{:S(2)}) copy-start(bf16[2,4,1024,64]{2,3,1,0:T(8,128)(2,1)} %get-tuple-element.55) | copy-start | bytes 3145732
  112.8 3.1 copy-start.4
  131.0 2.2 copy-start.2
  131.0 2.3 copy-start.7
  141.6 1.9 copy-start.3
  269.1 8.6 %copy-start.6 = (bf16[8,4,64,64]{2,3,1,0:T(8,128)(2,1)S(1)}, bf16[8,4,64,64]{2,3,1,0:T(8,128)(2,1)}, u32[]{:S(2)}) copy-start(bf16[8,4,64,64]{2,3,1,0:T(8,128)(2,1)} %get-tuple-element.68) | copy-start | bytes 786436
  273.8 50.6 %collective-permute-start.2 = (f32[2,4,512,128]{3,2,1,0:T(8,128)}, f32[2,4,512,128]{3,2,1,0:T(8,128)}, u32[]{:S(2)}, u32[]{:S(2)}) collective-permute-start(f32[2,4,512,128]{3,2,1,0:T(8,128)} %get-tuple-element.37), channel_id=1, source_target_pairs={{0,8},{8,16},{16,24},{24,0},{1,9},{9,17},{17,25},{25,1},{2,10},{10... | collective-permute-start | bytes 6291464 | tf_op jit(solution)/shard_map/ppermute | solution.py:23
  275.6 92.1 %collective-permute-start.3 = (f32[2,4,512,128]{3,2,1,0:T(8,128)}, f32[2,4,512,128]{3,2,1,0:T(8,128)}, u32[]{:S(2)}, u32[]{:S(2)}) collective-permute-start(f32[2,4,512,128]{3,2,1,0:T(8,128)} %get-tuple-element.36), channel_id=1, source_target_pairs={{8,0},{16,8},{24,16},{0,24},{9,1},{17,9},{25,17},{1,25},{10,2},{18... | collective-permute-start | bytes 6291464 | tf_op jit(solution)/shard_map/ppermute | solution.py:25
  278.6 104.3 %all-to-all-start.3 = ((bf16[8,64,256]{2,1,0:T(8,128)(2,1)}), bf16[8,64,256]{2,1,0:T(8,128)(2,1)S(1)}, u32[]{:S(2)}, u32[]{:S(2)}) async-start(bf16[8,64,256]{2,1,0:T(8,128)(2,1)} %copy.186), calls=%async_computation.3 | async-start | bytes 524288 | tf_op jit(solution)/shard_map/all_to_all | solution.py:217
  372.0 3.8 copy-start.12
  375.9 3.5 copy-start.10
  382.9 10.5 %all-to-all-start.5 = ((bf16[8,64,256]{2,1,0:T(8,128)(2,1)}), bf16[8,64,256]{2,1,0:T(8,128)(2,1)S(1)}, u32[]{:S(2)}, u32[]{:S(2)}) async-start(bf16[8,64,256]{2,1,0:T(8,128)(2,1)} %reshape.440), calls=%async_computation.5 | async-start | bytes 524288 | tf_op jit(solution)/shard_map/all_to_all | solution.py:218
  393.4 30.2 %all-to-all-start.6 = ((f32[2,8,128,256]{2,3,0,1:T(8,128)}), f32[2,8,128,256]{2,3,0,1:T(8,128)S(1)}, u32[]{:S(2)}, u32[]{:S(2)}) async-start(f32[2,8,128,256]{2,3,0,1:T(8,128)} %copy.210), calls=%async_computation.6 | async-start | bytes 4194304 | tf_op jit(solution)/shard_map/all_to_all | solution.py:205
  397.2 28.8 %copy-start.1 = (s32[1,8,8]{2,1,0:T(8,128)S(1)}, s32[1,8,8]{2,1,0:T(8,128)}, u32[]{:S(2)}) copy-start(s32[1,8,8]{2,1,0:T(8,128)} %param.11) | copy-start | bytes 772
where the time goes:
time: 434 us; the launch traced here: 426 us
  local copies, waits for them, and re-layouts  176 us (41%)
  waiting for transfers between devices  144 us (33%)
  other arithmetic  48.4 us (11%)
  starting transfers between devices  35.2 us (8%)
  matrix products  21 us (5%)
    ppermute x2, waiting for transfers between devices, with_halo(): lax.ppermute(tail, axis, [(i, (i + 1) % count) for i in range(count)])  54 us
    ppermute x2, waiting for transfers between devices, with_halo(): lax.ppermute(head, axis, [((i + 1) % count, i) for i in range(count)])  42.7 us
    all_to_all x1, waiting for transfers between devices, body(): lax.all_to_all(inner.reshape(2, seq_count, galaxies, pair_width), 'seq',...  24.6 us
    reshape x2, local copies, waits for them, and re-layouts, attend_group(): key_part.reshape(heads, group_size * neighbours, block_len, depth)  21.1 us
    reshape x2, local copies, waits for them, and re-layouts, attend_group(): value_part.reshape(heads, group_size * neighbours, block_len, depth)  20.8 us
    scatter-add x1, other arithmetic, attend_group(): value_acc.at[:, flat_ids]  13.4 us
    scatter-add x1, other arithmetic, attend_group(): key_acc.at[:, flat_ids]  13.2 us
    slice x2, local copies, waits for them, and re-layouts, body(): rim_out = accum[:, :, region_rows:].reshape(2, pair_heads, rim_rows, 2 * HD)  11.6 us
  transfers between devices with their start and end apart: 11, of which 9 were waited for; matrix products, arithmetic and copies ran while one was open for 16% of the time, Pallas kernels for 0%

commit v1 on v0

--- a/solution.py
+++ b/solution.py
@@ -4,6 +4,8 @@
 import jax
 import jax.numpy as jnp
 from jax import lax
+from jax.experimental import pallas as pl
+from jax.experimental.pallas import tpu as pltpu
 from jax.sharding import PartitionSpec as P
 
 H = 16
@@ -87,7 +89,7 @@
     return ((key_acc, value_acc), (attended, query_grad))
 
 
-def body(queries, keys, values, out_grad, table, counts, sendlist):
+def paired_body(queries, keys, values, out_grad, table, counts, sendlist):
     seq_count = lax.axis_size("seq")
     region_count = lax.axis_size("region")
     galaxies, width = queries.shape
@@ -229,7 +231,177 @@
     return (owner_rows(attended_back), owner_rows(qgrad_back), grads[0], grads[1])
 
 
+def attend_kernel(ids_ref, live_ref, counts_ref, q_ref, g_ref, own_ref, left_ref, right_ref,
+                  att_ref, qg_ref, own_acc, left_out, right_out, ext, acc, *, blocks, heads):
+    width = q_ref.shape[1]
+    rows = blocks * BLK
+    scale = 1.0 / math.sqrt(HD)
+    for part in range(2):
+        ext[part, :rows] = own_ref[part]
+        ext[part, rows:2 * rows] = left_ref[part]
+        ext[part, 2 * rows:] = right_ref[part]
+    acc[...] = jnp.zeros_like(acc)
+    lane_head = lax.broadcasted_iota(jnp.int32, (BLK, width), 1) // HD
+    row_pos = lax.broadcasted_iota(jnp.int32, (BLK, width), 0)
+    feat_head = lax.broadcasted_iota(jnp.int32, (width, BLK), 0) // HD
+    query_lane = lax.broadcasted_iota(jnp.int32, (width, BLK), 1)
+    key_pos = lax.broadcasted_iota(jnp.int32, (BLK, heads * BLK), 0)
+
+    def stacked(block):
+        return jnp.concatenate(
+            [jnp.where(lane_head == h, block, 0.0) for h in range(heads)], axis=0
+        ).astype(jnp.bfloat16)
+
+    def unstacked(wide):
+        out = wide[:, :BLK]
+        for h in range(1, heads):
+            out = jnp.where(feat_head == h, wide[:, h * BLK:(h + 1) * BLK], out)
+        return out
+
+    def one_block(b, carry):
+        here = pl.ds(pl.multiple_of(b * BLK, BLK), BLK)
+        count = counts_ref[b]
+        slots = [
+            pl.ds(pl.multiple_of(ids_ref[b * NBR + j] * BLK, BLK), BLK) for j in range(NBR)
+        ]
+        q_all = stacked(q_ref[here, :].astype(jnp.float32) * scale)
+        grad = jnp.where(row_pos < count, g_ref[here, :].astype(jnp.float32), 0.0)
+        g_all = stacked(grad)
+        k = jnp.concatenate([ext[0, s, :] for s in slots], axis=0)
+        v = jnp.concatenate([ext[1, s, :] for s in slots], axis=0)
+        scores = lax.dot_general(
+            k, q_all, (((1,), (1,)), ((), ())), preferred_element_type=jnp.float32
+        )
+        scores = jnp.concatenate(
+            [
+                jnp.where(
+                    key_pos < live_ref[b * NBR + j],
+                    scores[j * BLK:(j + 1) * BLK],
+                    jnp.float32(-1e30),
+                )
+                for j in range(NBR)
+            ],
+            axis=0,
+        )
+        peak = jnp.max(scores, axis=0, keepdims=True)
+        expo = jnp.exp(scores - peak)
+        inverse = 1.0 / jnp.sum(expo, axis=0, keepdims=True)
+        prob = (expo * inverse).astype(jnp.bfloat16)
+        att_wide = lax.dot_general(
+            v, prob, (((0,), (0,)), ((), ())), preferred_element_type=jnp.float32
+        )
+        att = unstacked(att_wide)
+        att = jnp.where(query_lane < count, att, 0.0).astype(jnp.bfloat16).astype(jnp.float32)
+        att_ref[here, :] = att.T.astype(jnp.bfloat16)
+        prod = grad.T * att
+        delta = jnp.concatenate(
+            [
+                jnp.sum(prod[h * HD:(h + 1) * HD], axis=0, keepdims=True)
+                for h in range(heads)
+            ],
+            axis=1,
+        )
+        dprob = lax.dot_general(
+            v, g_all, (((1,), (1,)), ((), ())), preferred_element_type=jnp.float32
+        )
+        dscore = (prob.astype(jnp.float32) * (dprob - delta)).astype(jnp.bfloat16)
+        qg_wide = lax.dot_general(
+            k, dscore, (((0,), (0,)), ((), ())), preferred_element_type=jnp.float32
+        )
+        qg_ref[here, :] = (unstacked(qg_wide).T * scale).astype(jnp.bfloat16)
+        dk = jnp.dot(dscore, q_all, preferred_element_type=jnp.float32)
+        dv = jnp.dot(prob, g_all, preferred_element_type=jnp.float32)
+        for j in range(NBR):
+            acc[0, slots[j], :] += dk[j * BLK:(j + 1) * BLK]
+            acc[1, slots[j], :] += dv[j * BLK:(j + 1) * BLK]
+        return carry
+
+    lax.fori_loop(0, blocks, one_block, 0)
+    for part in range(2):
+        own_acc[part] = acc[part, :rows]
+        left_out[part] = acc[part, rows:2 * rows].astype(jnp.bfloat16)
+        right_out[part] = acc[part, 2 * rows:].astype(jnp.bfloat16)
+
+
+def slab_ids(table, counts, sendlist, region_now, region_count, blocks):
+    left = (region_now + region_count - 1) % region_count
+    right = (region_now + 1) % region_count
+    remap = jnp.concatenate(
+        [
+            jnp.arange(blocks, dtype=jnp.int32),
+            blocks + sendlist[left, 1],
+            2 * blocks + sendlist[right, 0],
+        ]
+    )
+    slab_counts = jnp.concatenate([counts[region_now], counts[left], counts[right]])
+    ids = remap[jnp.maximum(table[0], 0)]
+    live = jnp.where(table[0] >= 0, slab_counts[ids], 0)
+    return ids.reshape(-1), live.reshape(-1), counts[region_now]
+
+
+def head_body(queries, keys, values, out_grad, table, counts, sendlist):
+    seq_count = lax.axis_size("seq")
+    region_count = lax.axis_size("region")
+    galaxies, features = queries.shape
+    width = features // seq_count
+    heads = width // HD
+    rows = seq_count * galaxies
+    blocks = rows // BLK
+    region_now = lax.axis_index("region")
+    ids, live, my_counts = slab_ids(table, counts, sendlist, region_now, region_count, blocks)
+
+    def to_heads(first, second):
+        pair = jnp.stack([first, second]).reshape(2, galaxies, seq_count, width)
+        sent = lax.all_to_all(
+            pair.transpose(2, 0, 1, 3), "seq", split_axis=0, concat_axis=0, tiled=True
+        )
+        return sent.transpose(1, 0, 2, 3).reshape(2, rows, width)
+
+    def to_rows(first, second):
+        pair = jnp.stack([first, second]).reshape(2, seq_count, galaxies, width)
+        sent = lax.all_to_all(
+            pair.transpose(1, 0, 2, 3), "seq", split_axis=0, concat_axis=0, tiled=True
+        )
+        return sent.transpose(1, 2, 0, 3).reshape(2, galaxies, features)
+
+    up = [(i, (i + 1) % region_count) for i in range(region_count)]
+    down = [((i + 1) % region_count, i) for i in range(region_count)]
+    own = to_heads(keys, values)
+    left = lax.ppermute(own, "region", up)
+    right = lax.ppermute(own, "region", down)
+    query_grad_in = to_heads(queries, out_grad)
+    vmem = pl.BlockSpec(memory_space=pltpu.VMEM)
+    smem = pl.BlockSpec(memory_space=pltpu.SMEM)
+    slab = jax.ShapeDtypeStruct((2, rows, width), jnp.bfloat16)
+    flat = jax.ShapeDtypeStruct((rows, width), jnp.bfloat16)
+    attended, query_grad, inner, to_left, to_right = pl.pallas_call(
+        partial(attend_kernel, blocks=blocks, heads=heads),
+        out_shape=(flat, flat, jax.ShapeDtypeStruct((2, rows, width), jnp.float32), slab, slab),
+        in_specs=[smem] * 3 + [vmem] * 5,
+        out_specs=[vmem] * 5,
+        scratch_shapes=[
+            pltpu.VMEM((2, 3 * rows, width), jnp.bfloat16),
+            pltpu.VMEM((2, 3 * rows, width), jnp.float32),
+        ],
+        compiler_params=pltpu.CompilerParams(vmem_limit_bytes=40 * 1024 * 1024),
+    )(ids, live, my_counts, query_grad_in[0], query_grad_in[1], own, left, right)
+    from_right = lax.ppermute(to_left, "region", down)
+    from_left = lax.ppermute(to_right, "region", up)
+    front = to_rows(attended, query_grad)
+    total = inner + from_right.astype(jnp.float32) + from_left.astype(jnp.float32)
+    total = total.astype(jnp.bfloat16)
+    grads = to_rows(total[0], total[1])
+    return (front[0], front[1], grads[0], grads[1])
+
+
 def solution(mesh):
+    whole_heads = H % mesh.shape["seq"] == 0
+
+    def body(queries, *rest):
+        blocks = mesh.shape["seq"] * queries.shape[0] // BLK
+        form = head_body if whole_heads and blocks == BND else paired_body
+        return form(queries, *rest)
+
     return jax.shard_map(
         body,
         mesh=mesh,

time: 434 us -> 106 us (0.24); the launches traced: 426 us -> 105 us
  local copies, waits for them, and re-layouts: 176 us -> 12 us
  waiting for transfers between devices: 144 us -> 53.7 us
  other arithmetic: 48.4 us -> 2.02 us
  matrix products: 21 us -> 0 us
  Pallas kernels: 0 us -> 15 us
  starting transfers between devices: 35.2 us -> 21.9 us
    reshape x25 -> x1, local copies, waits for them, and re-layouts: 87.2 us -> 0.83 us  [to_rows(): pair = jnp.stack([first, second]).reshape(2, seq_count, galaxies, width)]
    ppermute x4, waiting for transfers between devices: 96.6 us -> 36.1 us  [the longest x1 18.1 us: head_body(): from_right = lax.ppermute(to_left, 'region', down)]
    scatter-add x4 -> x0, other arithmetic: 33.5 us -> none  [the longest x1 13.4 us: attend_group(): value_acc.at[:, flat_ids]]
    all_to_all x7 -> x4, waiting for transfers between devices: 47.3 us -> 17.6 us  [the longest x2 9.9 us: to_heads(): lax.all_to_all(pair.transpose(2, 0, 1, 3), 'seq', split_axis=0, concat_ax...]
    dot_general x6 -> x0, matrix products: 21 us -> none  [the longest x1 6.66 us: attend_group(): jnp.einsum('bhqe,hbke->bhqk', query_grp, key_rows, preferred_element_type...]
    slice x8 -> x3, local copies, waits for them, and re-layouts: 18.4 us -> 0.13 us  [the longest x2 0.09 us: head_body(): return (front[0], front[1], grads[0], grads[1])]
    pallas_call x0 -> x1, Pallas kernels: none -> 15 us  [head_body(): pl.pallas_call(partial(attend_kernel, blocks=blocks, heads=heads), out_sh...]
    all_to_all x7 -> x4, starting transfers between devices: 27.8 us -> 16.3 us  [the longest x2 8.82 us: to_heads(): lax.all_to_all(pair.transpose(2, 0, 1, 3), 'seq', split_axis=0, concat_ax...]
  transfers between devices with their start and end apart: 11 -> 8, of which waited for: 9 -> 6; matrix products, arithmetic and copies ran while one was open for 16% -> 8% of each run, Pallas kernels for 0% -> 0%
where the time goes in v1:
time: 106 us; the launch traced here: 105 us
  waiting for transfers between devices  53.7 us (51%)
  starting transfers between devices  21.9 us (21%)
  Pallas kernels  15 us (14%)
  local copies, waits for them, and re-layouts  12 us (11%)
  other arithmetic  2.02 us (2%)
    ppermute x1, waiting for transfers between devices, head_body(): from_right = lax.ppermute(to_left, 'region', down)  18.1 us
    pallas_call x1, Pallas kernels, head_body(): pl.pallas_call(partial(attend_kernel, blocks=blocks, heads=heads), out_sh...  15 us
    ppermute x1, waiting for transfers between devices, head_body(): left = lax.ppermute(own, 'region', up)  11.5 us
    all_to_all x2, waiting for transfers between devices, to_heads(): lax.all_to_all(pair.transpose(2, 0, 1, 3), 'seq', split_axis=0, concat_ax...  9.9 us
    all_to_all x2, starting transfers between devices, to_heads(): lax.all_to_all(pair.transpose(2, 0, 1, 3), 'seq', split_axis=0, concat_ax...  8.82 us
    all_to_all x2, waiting for transfers between devices, to_rows(): lax.all_to_all(pair.transpose(1, 0, 2, 3), 'seq', split_axis=0, concat_ax...  7.68 us
    all_to_all x2, starting transfers between devices, to_rows(): lax.all_to_all(pair.transpose(1, 0, 2, 3), 'seq', split_axis=0, concat_ax...  7.43 us
    unnamed x18, local copies, waits for them, and re-layouts  6.52 us
  transfers between devices with their start and end apart: 8, of which 6 were waited for; matrix products, arithmetic and copies ran while one was open for 8% of the time, Pallas kernels for 0%

profile of v1, /device:TPU:0, one launch (start us, length us, event | category | flops | bytes accessed | tf_op | source)
XLA Modules:
  0.0 105.4 jit_solution(16135182818249317492)
XLA Ops:
  0.6 0.0 copy-start
  0.6 1.2 %copy.34 = bf16[128,1024]{0,1:T(8,128)(2,1)S(1)} copy(bf16[128,1024]{1,0:T(8,128)(2,1)} %param.8) | data formatting | bytes 524288 | tf_op args[1]
  1.8 0.0 copy-done
  1.8 0.2 copy.35
  2.0 0.1 maximum_bitcast_fusion.1
  2.0 1.0 copy.36
  3.1 0.0 copy-start.1
  3.1 5.3 %all-to-all-start.1 = ((bf16[8,2,128,128]{3,2,1,0:T(8,128)(2,1)}), bf16[8,2,128,128]{3,2,1,0:T(8,128)(2,1)S(1)}, u32[]{:S(2)}, u32[]{:S(2)}) async-start(bf16[8,2,128,128]{3,2,1,0:T(8,128)(2,1)} %copy.36), calls=%async_computation.1 | async-start | bytes 1048576 | tf_op jit(solution)/shard_map/all_to_all | solution.py:355
  8.4 0.0 copy-start.3
  8.4 0.7 copy-done.3
  9.1 0.1 reshape.86
  9.2 0.0 copy-done.1
  9.2 0.0 copy-start.2
  9.2 0.2 copy.31
  9.4 0.8 copy-done.2
  10.1 0.2 copy.32
  10.3 0.1 maximum_bitcast_fusion
  10.4 0.7 fusion.1
  11.1 0.1 pad_add_fusion
  11.2 0.8 gather_fusion
  11.9 0.1 gather.11
  12.0 1.0 copy.33
  13.1 0.0 copy-start.4
  13.1 5.0 %all-to-all-done.1 = bf16[8,2,128,128]{3,2,1,0:T(8,128)(2,1)S(1)} async-done(((bf16[8,2,128,128]{3,2,1,0:T(8,128)(2,1)}), bf16[8,2,128,128]{3,2,1,0:T(8,128)(2,1)S(1)}, u32[]{:S(2)}, u32[]{:S(2)}) %all-to-all-start.1) | async-done | bytes 524320 | tf_op jit(solution)/shard_map/all_to_all | solution.py:355
  18.1 3.5 %all-to-all-start = ((bf16[8,2,128,128]{3,2,1,0:T(8,128)(2,1)}), bf16[8,2,128,128]{3,2,1,0:T(8,128)(2,1)S(1)}, u32[]{:S(2)}, u32[]{:S(2)}) async-start(bf16[8,2,128,128]{3,2,1,0:T(8,128)(2,1)} %copy.33), calls=%async_computation | async-start | bytes 1048576 | tf_op jit(solution)/shard_map/all_to_all | solution.py:355
  21.6 0.0 copy-done.4
  21.6 0.1 reshape.94
  21.8 3.7 %collective-permute-start.1 = (bf16[2,1024,128]{2,1,0:T(8,128)(2,1)S(1)}, bf16[2,1024,128]{2,1,0:T(8,128)(2,1)S(1)}, u32[]{:S(2)}, u32[]{:S(2)}) collective-permute-start(bf16[2,1024,128]{2,1,0:T(8,128)(2,1)S(1)} %bitcast.43), channel_id=1, source_target_pairs={{8,0},{16,8},{24,16},{0,24},{9,1},{17,9},{25,17},{1,25},{10,2},{18... | collective-permute-start | bytes 1572872 | tf_op jit(solution)/shard_map/ppermute | solution.py:371
  25.4 0.0 collective-permute-start
  25.4 0.1 pad_add_fusion.1
  25.5 0.1 ge.8
  25.6 0.8 gather_fusion.1
  26.4 4.9 %all-to-all-done = bf16[8,2,128,128]{3,2,1,0:T(8,128)(2,1)S(1)} async-done(((bf16[8,2,128,128]{3,2,1,0:T(8,128)(2,1)}), bf16[8,2,128,128]{3,2,1,0:T(8,128)(2,1)S(1)}, u32[]{:S(2)}, u32[]{:S(2)}) %all-to-all-start) | async-done | bytes 524320 | tf_op jit(solution)/shard_map/all_to_all | solution.py:355
  31.3 6.5 %collective-permute-done.1.right_ref = bf16[2,1024,128]{2,1,0:T(8,128)(2,1)S(1)} collective-permute-done((bf16[2,1024,128]{2,1,0:T(8,128)(2,1)S(1)}, bf16[2,1024,128]{2,1,0:T(8,128)(2,1)S(1)}, u32[]{:S(2)}, u32[]{:S(2)}) %collective-permute-start.1) | collective-permute-done | bytes 524320 | tf_op jit(solution)/shard_map/ppermute | solution.py:371
  37.8 11.5 %collective-permute-done.left_ref = bf16[2,1024,128]{2,1,0:T(8,128)(2,1)S(1)} collective-permute-done((bf16[2,1024,128]{2,1,0:T(8,128)(2,1)S(1)}, bf16[2,1024,128]{2,1,0:T(8,128)(2,1)S(1)}, u32[]{:S(2)}, u32[]{:S(2)}) %collective-permute-start) | collective-permute-done | bytes 524320 | tf_op jit(solution)/shard_map/ppermute | solution.py:370
  49.3 15.0 %shard_map.102 = (bf16[1024,128]{1,0:T(8,128)(2,1)S(1)}, bf16[1024,128]{1,0:T(8,128)(2,1)S(1)}, f32[2,1024,128]{2,1,0:T(8,128)S(1)}, bf16[2,1024,128]{2,1,0:T(8,128)(2,1)}, bf16[2,1024,128]{2,1,0:T(8,128)(2,1)S(1)}) custom-call(s32[64]{0:T(128)S(1)} %gather_fusion, s32[64]{0:T(128)S(1)} %broadcast_select_fusion.live_ref, s32[8]{0:T(128)S(1)} %get-tuple-element.26.counts_ref, ...), custom_call_target="tpu_custom_call" | custom-call | tf_op jit(solution)/shard_map/pallas_call | solution.py:377
  64.3 1.7 %collective-permute-start.2 = (bf16[2,1024,128]{2,1,0:T(8,128)(2,1)}, bf16[2,1024,128]{2,1,0:T(8,128)(2,1)S(1)}, u32[]{:S(2)}, u32[]{:S(2)}) collective-permute-start(bf16[2,1024,128]{2,1,0:T(8,128)(2,1)} %get-tuple-element.12), channel_id=1, source_target_pairs={{8,0},{16,8},{24,16},{0,24},{9,1},{17,9},{25,17},{1,25},{10,2},{18... | collective-permute-start | bytes 1572872 | tf_op jit(solution)/shard_map/ppermute | solution.py:388
  66.0 0.3 collective-permute-start.3
  66.3 0.9 maximum_bitcast_fusion.2
  67.2 3.8 %all-to-all-start.2 = ((bf16[8,2,128,128]{3,2,1,0:T(8,128)(2,1)}), bf16[8,2,128,128]{3,2,1,0:T(8,128)(2,1)S(1)}, u32[]{:S(2)}, u32[]{:S(2)}) async-start(bf16[8,2,128,128]{3,2,1,0:T(8,128)(2,1)} %maximum_bitcast_fusion.2), calls=%async_computation.2 | async-start | bytes 1048576 | tf_op jit(solution)/shard_map/all_to_all | solution.py:362
  71.0 18.1 %collective-permute-done.2 = bf16[2,1024,128]{2,1,0:T(8,128)(2,1)S(1)} collective-permute-done((bf16[2,1024,128]{2,1,0:T(8,128)(2,1)}, bf16[2,1024,128]{2,1,0:T(8,128)(2,1)S(1)}, u32[]{:S(2)}, u32[]{:S(2)}) %collective-permute-start.2) | collective-permute-done | bytes 524320 | tf_op jit(solution)/shard_map/ppermute | solution.py:388
  89.1 0.0 collective-permute-done.3
  89.1 0.2 add_convert_fusion
  89.3 0.8 copy.48
  90.1 0.0 all-to-all-done.2
  90.1 3.6 %all-to-all-start.3 = ((bf16[8,2,128,128]{3,2,1,0:T(8,128)(2,1)}), bf16[8,2,128,128]{3,2,1,0:T(8,128)(2,1)S(1)}, u32[]{:S(2)}, u32[]{:S(2)}) async-start(bf16[8,2,128,128]{3,2,1,0:T(8,128)(2,1)} %bitcast.42), calls=%async_computation.3 | async-start | bytes 1048576 | tf_op jit(solution)/shard_map/all_to_all | solution.py:362
  93.7 0.3 copy.40
  94.0 0.9 copy.44
  94.9 0.8 copy.43
  95.7 7.7 %all-to-all-done.3 = bf16[8,2,128,128]{3,2,1,0:T(8,128)(2,1)S(1)} async-done(((bf16[8,2,128,128]{3,2,1,0:T(8,128)(2,1)}), bf16[8,2,128,128]{3,2,1,0:T(8,128)(2,1)S(1)}, u32[]{:S(2)}, u32[]{:S(2)}) %all-to-all-start.3) | async-done | bytes 524320 | tf_op jit(solution)/shard_map/all_to_all | solution.py:362
  103.4 0.3 copy.42
  103.7 0.9 copy.46
  104.6 0.8 copy.45
  (12 shorter events, 0.2 us)
Async XLA Ops:
  0.6 1.2 %copy-start = (bf16[128,1024]{1,0:T(8,128)(2,1)S(1)}, bf16[128,1024]{1,0:T(8,128)(2,1)}, u32[]{:S(2)}) copy-start(bf16[128,1024]{1,0:T(8,128)(2,1)} %param.9) | copy-start | bytes 786436
  3.1 6.1 %copy-start.1 = (bf16[128,1024]{1,0:T(8,128)(2,1)S(1)}, bf16[128,1024]{1,0:T(8,128)(2,1)}, u32[]{:S(2)}) copy-start(bf16[128,1024]{1,0:T(8,128)(2,1)} %param.7) | copy-start | bytes 786436
  3.1 15.0 %all-to-all-start.1 = ((bf16[8,2,128,128]{3,2,1,0:T(8,128)(2,1)}), bf16[8,2,128,128]{3,2,1,0:T(8,128)(2,1)S(1)}, u32[]{:S(2)}, u32[]{:S(2)}) async-start(bf16[8,2,128,128]{3,2,1,0:T(8,128)(2,1)} %copy.36), calls=%async_computation.1 | async-start | bytes 1048576 | tf_op jit(solution)/shard_map/all_to_all | solution.py:355
  8.4 0.7 copy-start.3
  9.2 1.0 copy-start.2
  13.1 8.5 %copy-start.4 = (s32[4,8]{1,0:T(4,128)S(1)}, s32[4,8]{1,0:T(4,128)}, u32[]{:S(2)}) copy-start(s32[4,8]{1,0:T(4,128)} %param.12) | copy-start | bytes 388
  18.1 13.1 %all-to-all-start = ((bf16[8,2,128,128]{3,2,1,0:T(8,128)(2,1)}), bf16[8,2,128,128]{3,2,1,0:T(8,128)(2,1)S(1)}, u32[]{:S(2)}, u32[]{:S(2)}) async-start(bf16[8,2,128,128]{3,2,1,0:T(8,128)(2,1)} %copy.33), calls=%async_computation | async-start | bytes 1048576 | tf_op jit(solution)/shard_map/all_to_all | solution.py:355
  21.8 16.0 %collective-permute-start.1 = (bf16[2,1024,128]{2,1,0:T(8,128)(2,1)S(1)}, bf16[2,1024,128]{2,1,0:T(8,128)(2,1)S(1)}, u32[]{:S(2)}, u32[]{:S(2)}) collective-permute-start(bf16[2,1024,128]{2,1,0:T(8,128)(2,1)S(1)} %bitcast.43), channel_id=1, source_target_pairs={{8,0},{16,8},{24,16},{0,24},{9,1},{17,9},{25,17},{1,25},{10,2},{18... | collective-permute-start | bytes 1572872 | tf_op jit(solution)/shard_map/ppermute | solution.py:371
  25.4 23.9 %collective-permute-start = (bf16[2,1024,128]{2,1,0:T(8,128)(2,1)S(1)}, bf16[2,1024,128]{2,1,0:T(8,128)(2,1)S(1)}, u32[]{:S(2)}, u32[]{:S(2)}) collective-permute-start(bf16[2,1024,128]{2,1,0:T(8,128)(2,1)S(1)} %bitcast.44), channel_id=1, source_target_pairs={{0,8},{8,16},{16,24},{24,0},{1,9},{9,17},{17,25},{25,1},{2,10},{10... | collective-permute-start | bytes 1572872 | tf_op jit(solution)/shard_map/ppermute | solution.py:370
  64.3 24.8 %collective-permute-start.2 = (bf16[2,1024,128]{2,1,0:T(8,128)(2,1)}, bf16[2,1024,128]{2,1,0:T(8,128)(2,1)S(1)}, u32[]{:S(2)}, u32[]{:S(2)}) collective-permute-start(bf16[2,1024,128]{2,1,0:T(8,128)(2,1)} %get-tuple-element.12), channel_id=1, source_target_pairs={{8,0},{16,8},{24,16},{0,24},{9,1},{17,9},{25,17},{1,25},{10,2},{18... | collective-permute-start | bytes 1572872 | tf_op jit(solution)/shard_map/ppermute | solution.py:388
  66.0 23.1 %collective-permute-start.3 = (bf16[2,1024,128]{2,1,0:T(8,128)(2,1)S(1)}, bf16[2,1024,128]{2,1,0:T(8,128)(2,1)S(1)}, u32[]{:S(2)}, u32[]{:S(2)}) collective-permute-start(bf16[2,1024,128]{2,1,0:T(8,128)(2,1)S(1)} %get-tuple-element.13), channel_id=1, source_target_pairs={{0,8},{8,16},{16,24},{24,0},{1,9},{9,17},{17,25},{25,1},{2,10},{10... | collective-permute-start | bytes 1572872 | tf_op jit(solution)/shard_map/ppermute | solution.py:389
  67.2 22.9 %all-to-all-start.2 = ((bf16[8,2,128,128]{3,2,1,0:T(8,128)(2,1)}), bf16[8,2,128,128]{3,2,1,0:T(8,128)(2,1)S(1)}, u32[]{:S(2)}, u32[]{:S(2)}) async-start(bf16[8,2,128,128]{3,2,1,0:T(8,128)(2,1)} %maximum_bitcast_fusion.2), calls=%async_computation.2 | async-start | bytes 1048576 | tf_op jit(solution)/shard_map/all_to_all | solution.py:362
  90.1 13.3 %all-to-all-start.3 = ((bf16[8,2,128,128]{3,2,1,0:T(8,128)(2,1)}), bf16[8,2,128,128]{3,2,1,0:T(8,128)(2,1)S(1)}, u32[]{:S(2)}, u32[]{:S(2)}) async-start(bf16[8,2,128,128]{3,2,1,0:T(8,128)(2,1)} %bitcast.42), calls=%async_computation.3 | async-start | bytes 1048576 | tf_op jit(solution)/shard_map/all_to_all | solution.py:362
